TPU v7x, 128 devices: a whole 4x4x4 slice. The times are simulated.
128 devices in a mesh: ctx: 8 (over x, z_lo), fsdp: 16 (over z_hi, y, core).
Axes of the slice: x: 4, y: 4, z: 4 (z_hi: 2, z_lo: 2; z = z_hi * 2 + z_lo), core: 2. Of those that a mesh axis runs over, the one named last changes fastest.
Arguments:
- inputs: bfloat16 [16, 1024, 1152], P('fsdp', 'ctx'), may hold values from -6 to 6
- out_grad: bfloat16 [16, 1024, 1152], P('fsdp', 'ctx'), may hold values from -6 to 6
- positions: int32 [16, 1024], P('fsdp', 'ctx'), may hold values from 0 to 1023, as said below
- block_order: int32 [8, 2], replicated, may hold values from 0 to 15, as said below
- w_query: bfloat16 [1152, 1024], P('fsdp'), may hold values from -0.1875 to 0.1875
- w_key: bfloat16 [1152, 256], P('fsdp'), may hold values from -0.1875 to 0.1875
- w_value: bfloat16 [1152, 256], P('fsdp'), may hold values from -0.1875 to 0.1875
- w_output: bfloat16 [1024, 1152], P(None, 'fsdp'), may hold values from -0.1875 to 0.1875
- w_gate: bfloat16 [6912, 1152], P('fsdp'), may hold values from -0.1875 to 0.1875
- w_up: bfloat16 [6912, 1152], P('fsdp'), may hold values from -0.1875 to 0.1875
- w_down: bfloat16 [6912, 1152], P('fsdp'), may hold values from -0.078125 to 0.078125
- gain_in: bfloat16 [1152], P('fsdp'), may hold values from 0.099609375 to 1.8984375
- gain_query: bfloat16 [256], P('fsdp'), may hold values from 0.099609375 to 1.8984375
- gain_key: bfloat16 [256], P('fsdp'), may hold values from 0.099609375 to 1.8984375
- gain_attn: bfloat16 [1152], P('fsdp'), may hold values from 0.099609375 to 1.8984375
- gain_pre: bfloat16 [1152], P('fsdp'), may hold values from 0.099609375 to 1.8984375
- gain_post: bfloat16 [1152], P('fsdp'), may hold values from 0.099609375 to 1.8984375
Outputs:
- outputs: bfloat16 [16, 1024, 1152], P('fsdp', 'ctx')
- in_grad: bfloat16 [16, 1024, 1152], P('fsdp', 'ctx')
- grad_w_query: float32 [1152, 1024], P('fsdp')
- grad_w_key: float32 [1152, 256], P('fsdp')
- grad_w_value: float32 [1152, 256], P('fsdp')
- grad_w_output: float32 [1024, 1152], P(None, 'fsdp')
- grad_w_gate: float32 [6912, 1152], P('fsdp')
- grad_w_up: float32 [6912, 1152], P('fsdp')
- grad_w_down: float32 [6912, 1152], P('fsdp')
- grad_gain_in: float32 [1152], P('fsdp')
- grad_gain_query: float32 [256], P('fsdp')
- grad_gain_key: float32 [256], P('fsdp')
- grad_gain_attn: float32 [1152], P('fsdp')
- grad_gain_pre: float32 [1152], P('fsdp')
- grad_gain_post: float32 [1152], P('fsdp')
Inputs may be any that keep to these rules, and one draw needn't show every extreme that they name: `block_order`: row c names the two blocks of 64 tokens in device c's rows, in order; every block appears once, and a row holds blocks k and m with k + m one less than the number of blocks. `positions`: each row's offset from the start of its document in the sequence; documents begin at the sequence's first token and at random places; sequence 0 is one document.
All inputs are finite; a program needn't handle non-finite values.
Results may differ from a plain program's by a relative error of at most 0.03.
Values may be sent and summed in bfloat16 or wider, within the bound.
No kernel may reach another device: no remote copies, remote signals or barrier semaphores. Data moves between devices by JAX's collectives and lax.ppermute only.
A program may use at most 128 MiB of HBM per device.

v0:
```python
import jax
import jax.numpy as jnp
from jax import lax
from jax.sharding import PartitionSpec as P

H = 4
HD = 256
EPS = 1e-06
ROPE_BASE = 1000000.0
GELU_C = 0.7978845608028654
GELU_A = 0.044715


def norm_forward(values, gain):
    inverse = lax.rsqrt(jnp.mean(values * values, axis=-1, keepdims=True) + EPS)
    unit = values * inverse
    return (unit * gain, unit, inverse)


def norm_backward(upstream, unit, inverse, gain):
    scaled = upstream * gain
    inner = jnp.mean(scaled * unit, axis=-1, keepdims=True)
    leading = tuple(range(upstream.ndim - 1))
    return (inverse * (scaled - unit * inner), jnp.sum(upstream * unit, axis=leading))


def gelu_pair(gate):
    inner = GELU_C * (gate + GELU_A * gate * gate * gate)
    tangent = jnp.tanh(inner)
    value = 0.5 * gate * (1.0 + tangent)
    slope = 0.5 * (1.0 + tangent) + 0.5 * gate * (1.0 - tangent * tangent) * GELU_C * (
        1.0 + 3.0 * GELU_A * gate * gate
    )
    return (value, slope)


def rope_tables(positions, width):
    half = width // 2
    freqs = ROPE_BASE ** (-2.0 * jnp.arange(half, dtype=jnp.float32) / width)
    angles = positions.astype(jnp.float32)[:, None] * freqs[None, :]
    return (jnp.cos(angles), jnp.sin(angles))


def rotate(values, cosine, sine):
    half = values.shape[-1] // 2
    first = values[..., :half]
    second = values[..., half:]
    return jnp.concatenate(
        [first * cosine - second * sine, second * cosine + first * sine], axis=-1
    )


def rotate_back(values, cosine, sine):
    half = values.shape[-1] // 2
    first = values[..., :half]
    second = values[..., half:]
    return jnp.concatenate(
        [first * cosine + second * sine, second * cosine - first * sine], axis=-1
    )


def sequence_rows(order_flat, first_row, count, block):
    rows = first_row + jnp.arange(count, dtype=jnp.int32)
    slots = rows // block
    table = jnp.arange(order_flat.shape[0], dtype=jnp.int32)
    picked = jnp.sum(jnp.where(slots[:, None] == table[None, :], order_flat[None, :], 0), axis=1)
    return picked * block + rows % block


def pad_rows(shard, rows):
    return jnp.pad(shard, (0, rows - shard.shape[0]))


def a2a_sum(x, axis_name, count):
    pieces = lax.all_to_all(x.reshape(count, -1, *x.shape[1:]), axis_name, 0, 0)
    return jnp.sum(pieces.astype(jnp.float32), axis=0)


def a2a_gather(x, axis_name, count):
    copies = jnp.broadcast_to(x[None], (count,) + x.shape)
    return lax.all_to_all(copies, axis_name, 0, 0).reshape(count * x.shape[0], *x.shape[1:])


def body(
    inputs,
    out_grad,
    positions,
    block_order,
    w_query,
    w_key,
    w_value,
    w_output,
    w_gate,
    w_up,
    w_down,
    gain_in,
    gain_query,
    gain_key,
    gain_attn,
    gain_pre,
    gain_post,
):
    f32 = jnp.float32
    low = jnp.bfloat16
    tokens = inputs[0]
    local = tokens.shape[0]
    parts = lax.axis_size("ctx")
    groups = lax.axis_size("fsdp")
    total = local * parts
    block = local // 2
    width_shard = w_query.shape[0]
    qw = w_query.shape[1]
    kw = w_key.shape[1]
    gain_cols = jnp.stack(
        [
            gain_in,
            gain_attn,
            gain_pre,
            gain_post,
            pad_rows(gain_query, width_shard),
            pad_rows(gain_key, width_shard),
        ],
        axis=1,
    )
    gain_cols = jnp.pad(gain_cols, ((0, 0), (0, 128 - gain_cols.shape[1])))
    packed = jnp.concatenate([w_query, w_key, w_value, w_output.T, gain_cols], axis=1)
    packed_all = lax.all_gather(packed, "fsdp", axis=0, tiled=True)
    o1 = qw
    o2 = o1 + kw
    o3 = o2 + kw
    o4 = o3 + w_output.shape[0]
    full_query = packed_all[:, :o1]
    full_key = packed_all[:, o1:o2]
    full_value = packed_all[:, o2:o3]
    full_output_t = packed_all[:, o3:o4]
    gains_all = packed_all[:, o4:].astype(f32)
    head_shard = gain_query.shape[0]

    def head_gain(col):
        return col.reshape(groups, width_shard)[:, :head_shard].reshape(-1)

    norm_in = gains_all[:, 0]
    norm_attn = gains_all[:, 1]
    norm_pre = gains_all[:, 2]
    norm_post = gains_all[:, 3]
    norm_query = head_gain(gains_all[:, 4])
    norm_key = head_gain(gains_all[:, 5])
    ctx_index = lax.axis_index("ctx")
    order_flat = block_order.reshape(-1)
    my_seq = sequence_rows(order_flat, ctx_index * local, local, block)
    all_seq = sequence_rows(order_flat, 0, total, block)
    flat_in = tokens.astype(f32)
    normed_full, unit_in, inv_in = norm_forward(flat_in, norm_in)
    normed_in = normed_full.astype(low)
    queries = jnp.dot(normed_in, full_query, preferred_element_type=f32).reshape(local, H, HD)
    keys_raw = jnp.dot(normed_in, full_key, preferred_element_type=f32)
    values = jnp.dot(normed_in, full_value, preferred_element_type=f32).astype(low)
    query_normed, query_unit, query_inv = norm_forward(queries, norm_query)
    key_normed, key_unit, key_inv = norm_forward(keys_raw, norm_key)
    cosine, sine = rope_tables(positions[0], HD)
    scale = HD ** (-0.5)
    query_rot = (rotate(query_normed, cosine[:, None, :], sine[:, None, :]) * scale).astype(low)
    key_rot = rotate(key_normed, cosine, sine).astype(low)
    kv_all = a2a_gather(jnp.concatenate([key_rot, values], axis=1), "ctx", parts)
    key_all = kv_all[:, :HD]
    value_all = kv_all[:, HD:]
    scores = jnp.einsum("qhd,kd->hqk", query_rot, key_all, preferred_element_type=f32)
    allowed = my_seq[:, None] >= all_seq[None, :]
    scores = jnp.where(allowed[None], scores, -jnp.inf)
    highest = jnp.max(scores, axis=-1, keepdims=True)
    log_total = highest + jnp.log(jnp.sum(jnp.exp(scores - highest), axis=-1, keepdims=True))
    probs_full = jnp.exp(scores - log_total)
    probs = probs_full.astype(low)
    attended = (
        jnp.einsum("hqk,kd->qhd", probs, value_all, preferred_element_type=f32)
        .reshape(local, H * HD)
        .astype(low)
    )
    branch_attn = jnp.einsum("tc,dc->td", attended, full_output_t, preferred_element_type=f32)
    attn_normed, attn_unit, attn_inv = norm_forward(branch_attn, norm_attn)
    residual = flat_in + attn_normed
    pre_full, pre_unit, pre_inv = norm_forward(residual, norm_pre)
    normed_pre = pre_full.astype(low)
    rows_all = lax.all_gather(normed_pre, "fsdp", axis=0, tiled=True)
    gate = jnp.einsum("td,fd->tf", rows_all, w_gate, preferred_element_type=f32)
    upper = jnp.einsum("td,fd->tf", rows_all, w_up, preferred_element_type=f32)
    gelu_value, gelu_slope = gelu_pair(gate)
    hidden = (gelu_value * upper).astype(low)
    branch_ffn = a2a_sum(
        jnp.dot(hidden, w_down, preferred_element_type=f32).astype(jnp.bfloat16), "fsdp", groups
    )
    post_normed, post_unit, post_inv = norm_forward(branch_ffn, norm_post)
    outputs = (residual + post_normed).astype(low)
    grad_out = out_grad[0].astype(f32)
    grad_ffn_full, grad_gain_post = norm_backward(grad_out, post_unit, post_inv, norm_post)
    grad_ffn = grad_ffn_full.astype(low)
    grad_all = a2a_gather(grad_ffn, "fsdp", groups)
    grad_hidden = jnp.einsum("td,fd->tf", grad_all, w_down, preferred_element_type=f32)
    grad_gate = (grad_hidden * upper * gelu_slope).astype(low)
    grad_up = (grad_hidden * gelu_value).astype(low)
    shard_gate = jnp.einsum("tf,td->fd", grad_gate, rows_all, preferred_element_type=f32)
    shard_up = jnp.einsum("tf,td->fd", grad_up, rows_all, preferred_element_type=f32)
    shard_down = jnp.einsum("tf,td->fd", hidden, grad_all, preferred_element_type=f32)
    grad_pre = a2a_sum(
        (
            jnp.dot(grad_gate, w_gate, preferred_element_type=f32)
            + jnp.dot(grad_up, w_up, preferred_element_type=f32)
        ).astype(jnp.bfloat16),
        "fsdp",
        groups,
    )
    grad_from_pre, grad_gain_pre = norm_backward(grad_pre, pre_unit, pre_inv, norm_pre)
    grad_residual = grad_out + grad_from_pre
    grad_branch_full, grad_gain_attn = norm_backward(grad_residual, attn_unit, attn_inv, norm_attn)
    grad_branch = grad_branch_full.astype(low)
    term_output = jnp.einsum("tc,td->cd", attended, grad_branch, preferred_element_type=f32)
    grad_attended = jnp.einsum(
        "td,dc->tc", grad_branch, full_output_t, preferred_element_type=f32
    ).astype(low)
    grad_heads = grad_attended.reshape(local, H, HD)
    attended_heads = attended.reshape(local, H, HD)
    delta = jnp.transpose(jnp.sum(grad_heads.astype(f32) * attended_heads.astype(f32), axis=-1))[
        :, :, None
    ]
    grad_probs = jnp.einsum("qhd,kd->hqk", grad_heads, value_all, preferred_element_type=f32)
    grad_scores = (probs_full * (grad_probs - delta)).astype(low)
    value_term = jnp.einsum("hqk,qhd->kd", probs, grad_heads, preferred_element_type=f32)
    key_term = jnp.einsum("hqk,qhd->kd", grad_scores, query_rot, preferred_element_type=f32)
    key_value_terms = jnp.concatenate([key_term, value_term], axis=1)
    grad_query_rot = jnp.einsum("hqk,kd->qhd", grad_scores, key_all, preferred_element_type=f32)
    summed_kv = a2a_sum(key_value_terms.astype(jnp.bfloat16), "ctx", parts)
    grad_key_rot = summed_kv[:, :HD]
    grad_values = summed_kv[:, HD:].astype(low)
    grad_q_normed = rotate_back(grad_query_rot * scale, cosine[:, None, :], sine[:, None, :])
    grad_q_full, grad_gain_query = norm_backward(grad_q_normed, query_unit, query_inv, norm_query)
    grad_k_normed = rotate_back(grad_key_rot, cosine, sine)
    grad_k_full, grad_gain_key = norm_backward(grad_k_normed, key_unit, key_inv, norm_key)
    grad_q_in = grad_q_full.reshape(local, H * HD).astype(low)
    grad_k_in = grad_k_full.astype(low)
    term_query = jnp.einsum("tc,td->cd", grad_q_in, normed_in, preferred_element_type=f32)
    term_key = jnp.einsum("tc,td->cd", grad_k_in, normed_in, preferred_element_type=f32)
    term_value = jnp.einsum("tc,td->cd", grad_values, normed_in, preferred_element_type=f32)
    grad_normed = (
        jnp.einsum("tc,dc->td", grad_q_in, full_query, preferred_element_type=f32)
        + jnp.einsum("tc,dc->td", grad_k_in, full_key, preferred_element_type=f32)
        + jnp.einsum("tc,dc->td", grad_values, full_value, preferred_element_type=f32)
    )
    grad_from_in, grad_gain_in = norm_backward(grad_normed, unit_in, inv_in, norm_in)
    in_grad = (grad_residual + grad_from_in).astype(low)

    def head_col(g):
        return jnp.pad(
            g.reshape(groups, head_shard), ((0, 0), (0, width_shard - head_shard))
        ).reshape(-1)

    gain_block = jnp.stack(
        [
            grad_gain_in,
            grad_gain_attn,
            grad_gain_pre,
            grad_gain_post,
            head_col(grad_gain_query),
            head_col(grad_gain_key),
        ],
        axis=0,
    )
    gain_block = jnp.pad(gain_block, ((0, 8 - gain_block.shape[0]), (0, 0))).astype(low)
    gain_block = jnp.transpose(gain_block.reshape(8, groups, width_shard), (1, 0, 2))
    gain_shard = jnp.sum(lax.all_to_all(gain_block, "fsdp", 0, 0).astype(f32), axis=0)

    def ctx_sum(x):
        chunks = x.reshape(parts, -1, x.shape[1])
        mine = jnp.sum(lax.all_to_all(chunks, "ctx", 0, 0).astype(f32), axis=0).astype(low)
        return lax.all_to_all(jnp.broadcast_to(mine[None], chunks.shape), "ctx", 0, 0).reshape(
            x.shape
        )

    ffn_units = shard_gate.shape[0]
    ffn_sums = ctx_sum(
        jnp.concatenate([shard_gate, shard_up, shard_down], axis=0).astype(low)
    ).astype(f32)
    grad_packed = jnp.concatenate([term_query, term_key, term_value, term_output], axis=0).astype(
        low
    )
    grad_shard = jnp.concatenate(
        [
            lax.psum_scatter(grad_packed, "fsdp", scatter_dimension=1, tiled=True),
            gain_shard.astype(low),
        ],
        axis=0,
    )
    totals = (
        ctx_sum(grad_shard),
        ffn_sums[:ffn_units],
        ffn_sums[ffn_units : 2 * ffn_units],
        ffn_sums[2 * ffn_units :],
    )
    grad_shard = totals[0].astype(f32)
    grows = grad_shard[o4:]
    return (
        outputs[None],
        in_grad[None],
        grad_shard[:o1].T,
        grad_shard[o1:o2].T,
        grad_shard[o2:o3].T,
        grad_shard[o3:o4],
        totals[1].astype(f32),
        totals[2].astype(f32),
        totals[3].astype(f32),
        grows[0],
        grows[4, :head_shard],
        grows[5, :head_shard],
        grows[1],
        grows[2],
        grows[3],
    )


def solution(mesh):
    placed = (
        P("fsdp", "ctx", None),
        P("fsdp", "ctx", None),
        P("fsdp", "ctx"),
        P(),
        P("fsdp", None),
        P("fsdp", None),
        P("fsdp", None),
        P(None, "fsdp"),
        P("fsdp", None),
        P("fsdp", None),
        P("fsdp", None),
        P("fsdp"),
        P("fsdp"),
        P("fsdp"),
        P("fsdp"),
        P("fsdp"),
        P("fsdp"),
    )
    return jax.shard_map(
        body,
        mesh=mesh,
        in_specs=placed,
        out_specs=(
            P("fsdp", "ctx", None),
            P("fsdp", "ctx", None),
            P("fsdp", None),
            P("fsdp", None),
            P("fsdp", None),
            P(None, "fsdp"),
            P("fsdp", None),
            P("fsdp", None),
            P("fsdp", None),
            P("fsdp"),
            P("fsdp"),
            P("fsdp"),
            P("fsdp"),
            P("fsdp"),
            P("fsdp"),
        ),
        check_vma=False,
    )
```

profile of v0, /device:TPU:0, one launch (start us, length us, event | category | flops | bytes accessed | tf_op | source)
XLA Modules:
  0.0 611.8 jit_solution(8419735347400589756)
XLA Ops:
  16.2 63.4 %all-gather.3.cloned.1.call-done = bf16[1152,2688]{1,0:T(8,128)(2,1)} async-done(((bf16[72,2688]{1,0:T(8,128)(2,1)}), bf16[1152,2688]{1,0:T(8,128)(2,1)}) %all-gather.3.cloned.1.call-update) | async-done | bytes 6193168 | tf_op jit(solution)/shard_map/all_gather | solution.py:127
  80.6 1.8 slice_reduce_fusion
  84.0 3.3 slice_bitcast_fusion
  87.3 4.3 copy.90
  94.8 4.3 all-to-all-start
  99.7 2.6 multiply_reduce_fusion.10
  103.4 12.4 %all-to-all-done = bf16[8,128,512]{2,1,0:T(8,128)(2,1)S(1)} async-done(((bf16[8,128,512]{2,1,0:T(8,128)(2,1)}), bf16[8,128,512]{2,1,0:T(8,128)(2,1)S(1)}, u32[]{:S(2)}, u32[]{:S(2)}) %all-to-all-start) | async-done | bytes 1048608 | tf_op jit(solution)/shard_map/all_to_all | solution.py:81
  118.4 2.7 multiply_reduce_fusion.6
  122.3 54.8 %all-gather.5.cloned.1.call-done = bf16[2048,1152]{1,0:T(8,128)(2,1)} async-done(((bf16[128,1152]{1,0:T(8,128)(2,1)}), bf16[2048,1152]{1,0:T(8,128)(2,1)}) %all-gather.5.cloned.1.call-update) | async-done | bytes 4718608 | tf_op jit(solution)/shard_map/all_gather | solution.py:184
  177.1 5.2 fusion.109
  182.3 2.9 multiply_convert_fusion.1
  185.3 3.2 convolution_convert_fusion
  188.5 60.9 %all_to_all.50 = bf16[16,128,1152]{2,1,0:T(8,128)(2,1)S(1)} all-to-all(bf16[16,128,1152]{2,1,0:T(8,128)(2,1)S(1)} %bitcast.206), channel_id=1, replica_groups=mesh['ctx'=8,'fsdp'=16] {'fsdp'}, dimensions={0} | all-to-all | bytes 9437184 | tf_op jit(solution)/shard_map/all_to_all | solution.py:75
  252.2 60.2 %all_to_all.51 = bf16[16,128,1152]{2,1,0:T(8,128)(2,1)S(1)} all-to-all(bf16[16,128,1152]{2,1,0:T(8,128)(2,1)S(1)} %broadcast_in_dim.66), channel_id=1, replica_groups=mesh['ctx'=8,'fsdp'=16] {'fsdp'}, dimensions={0} | all-to-all | bytes 9437184 | tf_op jit(solution)/shard_map/all_to_all | solution.py:81
  312.4 4.6 multiply_convert_fusion
  317.0 3.0 fusion.110
  320.0 4.8 add_convert_fusion
  324.8 4.6 all-to-all-start.3
  329.6 3.0 fusion.8
  332.6 60.1 %all-to-all-done.3 = bf16[16,128,1152]{2,1,0:T(8,128)(2,1)} async-done(((bf16[16,128,1152]{2,1,0:T(8,128)(2,1)}), bf16[16,128,1152]{2,1,0:T(8,128)(2,1)}, u32[]{:S(2)}, u32[]{:S(2)}) %all-to-all-start.3) | async-done | bytes 4718624 | tf_op jit(solution)/shard_map/all_to_all | solution.py:75
  392.7 3.1 convert_reduce_fusion
  398.7 2.9 fusion.22
  403.9 1.8 fusion.10
  409.2 5.2 all-to-all-start.4
  418.1 2.2 convolution_convert_fusion.1
  420.3 2.3 convolution_convert_fusion.2
  422.7 7.5 %all-to-all-done.4 = bf16[8,128,512]{2,1,0:T(8,128)(2,1)S(1)} async-done(((bf16[8,128,512]{2,1,0:T(8,128)(2,1)}), bf16[8,128,512]{2,1,0:T(8,128)(2,1)S(1)}, u32[]{:S(2)}, u32[]{:S(2)}) %all-to-all-start.4) | async-done | bytes 1048608 | tf_op jit(solution)/shard_map/all_to_all | solution.py:75
  431.8 4.6 pad_maximum_fusion
  436.5 8.9 %copy.117 = bf16[2560,1152]{0,1:T(8,128)(2,1)} copy(bf16[2560,1152]{1,0:T(8,128)(2,1)} %pad_maximum_fusion) | data formatting | bytes 11796480
  445.4 5.5 convolution_convert_fusion.3
  450.9 2.5 convolution_convert_fusion.4
  453.4 2.5 convolution_convert_fusion.5
  455.9 1.8 pad_maximum_fusion.1
  457.7 3.6 convert_element_type.207
  461.3 44.3 %all_to_all.52 = bf16[8,162,1152]{2,1,0:T(8,128)(2,1)} all-to-all(bf16[8,162,1152]{2,1,0:T(8,128)(2,1)} %convert_element_type.207), channel_id=1, replica_groups=mesh['ctx'=8,'fsdp'=16] {'ctx'}, dimensions={0} | all-to-all | bytes 5971968 | tf_op jit(solution)/shard_map/all_to_all | solution.py:273
  505.6 2.4 reduce_sum.291
  508.0 1.9 broadcast_in_dim.117
  509.9 5.1 all-to-all-start.9
  515.3 2.6 fusion.15
  521.9 35.5 %all-to-all-done.9 = bf16[8,162,1152]{2,1,0:T(8,128)(2,1)} async-done(((bf16[8,162,1152]{2,1,0:T(8,128)(2,1)}), bf16[8,162,1152]{2,1,0:T(8,128)(2,1)}, u32[]{:S(2)}, u32[]{:S(2)}) %all-to-all-start.9) | async-done | bytes 2986016 | tf_op jit(solution)/shard_map/all_to_all | solution.py:274
  557.4 8.7 %all-to-all-start.5 = ((bf16[16,8,72]{2,1,0:T(8,128)(2,1)}), bf16[16,8,72]{2,1,0:T(8,128)(2,1)S(1)}, u32[]{:S(2)}, u32[]{:S(2)}) async-start(bf16[16,8,72]{2,1,0:T(8,128)(2,1)} %copy.100), calls=%async_computation.5 | async-start | bytes 65536 | tf_op jit(solution)/shard_map/all_to_all | solution.py:269
  566.1 4.3 reshape.425
  570.4 3.3 all-to-all-done.5
  576.4 3.5 all-to-all-start.6
  579.9 5.5 fusion.107
  585.4 3.5 all-to-all-done.6
  589.8 3.5 all-to-all-start.7
  594.3 7.4 %all-to-all-done.7 = bf16[8,321,72]{1,2,0:T(8,128)(2,1)S(1)} async-done(((bf16[8,321,72]{1,2,0:T(8,128)(2,1)}), bf16[8,321,72]{1,2,0:T(8,128)(2,1)S(1)}, u32[]{:S(2)}, u32[]{:S(2)}) %all-to-all-start.7) | async-done | bytes 369824 | tf_op jit(solution)/shard_map/all_to_all | solution.py:274
  (212 shorter events, 48.5 us)
Async XLA Ops:
  7.2 178.1 %copy-start = (bf16[432,1152]{1,0:T(8,128)(2,1)S(1)}, bf16[432,1152]{1,0:T(8,128)(2,1)}, u32[]{:S(2)}) copy-start(bf16[432,1152]{1,0:T(8,128)(2,1)} %param.27) | copy-start | bytes 2985988
  7.2 75.2 %copy-start.2 = (bf16[1,128,1152]{2,1,0:T(8,128)(2,1)S(1)}, bf16[1,128,1152]{2,1,0:T(8,128)(2,1)}, u32[]{:S(2)}) copy-start(bf16[1,128,1152]{2,1,0:T(8,128)(2,1)} %param.17) | copy-start | bytes 884740
  7.2 72.4 %all-gather.3.cloned.1.call-start = ((), (), s32[]{:S(2)}) async-start(), calls=%async_computation.11 | async-start | bytes 6580224 | tf_op jit(solution)/shard_map/all_gather | solution.py:127
  13.9 78.0 %copy-start.35 = (f32[128]{0:T(128)}, f32[128]{0:T(128)S(1)}, u32[]{:S(2)}) copy-start(f32[128]{0:T(128)S(1)} %multiply_power_fusion) | copy-start | bytes 1540
  15.9 76.0 %copy-start.37 = (f32[128]{0:T(128)}, f32[128]{0:T(128)S(1)}, u32[]{:S(2)}) copy-start(f32[128]{0:T(128)S(1)} %convert_bitcast_fusion.2) | copy-start | bytes 1540
  16.2 100.7 %copy-start.25 = (pred[128,1024]{0,1:T(8,128)(4,1)}, pred[128,1024]{0,1:T(8,128)(4,1)S(1)}, u32[]{:S(2)}) copy-start(pred[128,1024]{0,1:T(8,128)(4,1)S(1)} %broadcast_compare_fusion.1) | copy-start | bytes 393220
  83.8 8.0 %copy-start.33 = (f32[128]{0:T(128)}, f32[128]{0:T(128)S(1)}, u32[]{:S(2)}) copy-start(f32[128]{0:T(128)S(1)} %add_rsqrt_fusion.4) | copy-start | bytes 1540
  92.3 11.0 %copy-start.21 = (f32[128,128]{1,0:T(8,128)}, f32[128,128]{1,0:T(8,128)S(1)}, u32[]{:S(2)}) copy-start(f32[128,128]{1,0:T(8,128)S(1)} %get-tuple-element.60) | copy-start | bytes 196612
  92.3 11.0 %copy-start.23 = (f32[128,128]{1,0:T(8,128)}, f32[128,128]{1,0:T(8,128)S(1)}, u32[]{:S(2)}) copy-start(f32[128,128]{1,0:T(8,128)S(1)} %get-tuple-element.61) | copy-start | bytes 196612
  94.8 21.1 %all-to-all-start = ((bf16[8,128,512]{2,1,0:T(8,128)(2,1)}), bf16[8,128,512]{2,1,0:T(8,128)(2,1)S(1)}, u32[]{:S(2)}, u32[]{:S(2)}) async-start(bf16[8,128,512]{2,1,0:T(8,128)(2,1)} %broadcast_in_dim.56), calls=%async_computation | async-start | bytes 2097152 | tf_op jit(solution)/shard_map/all_to_all | solution.py:81
  99.1 77.9 %all-gather.5.cloned.1.call-start = ((), (), s32[]{:S(2)}) async-start(), calls=%async_computation.12 | async-start | bytes 5013504 | tf_op jit(solution)/shard_map/all_gather | solution.py:184
  103.4 13.4 %copy-start.26 = (f32[128,4,128]{2,0,1:T(8,128)}, f32[128,4,128]{2,0,1:T(8,128)S(1)}, u32[]{:S(2)}) copy-start(f32[128,4,128]{2,0,1:T(8,128)S(1)} %get-tuple-element.53) | copy-start | bytes 786436
  103.4 14.9 %copy-start.28 = (f32[128,4,128]{2,0,1:T(8,128)}, f32[128,4,128]{2,0,1:T(8,128)S(1)}, u32[]{:S(2)}) copy-start(f32[128,4,128]{2,0,1:T(8,128)S(1)} %get-tuple-element.54) | copy-start | bytes 786436
  117.7 211.9 %copy-start.30 = (f32[4,128]{1,0:T(4,128)}, f32[4,128]{1,0:T(4,128)S(1)}, u32[]{:S(2)}) copy-start(f32[4,128]{1,0:T(4,128)S(1)} %log_add_fusion) | copy-start | bytes 6148
  118.3 64.0 %copy-start.16 = (bf16[256,4,128]{2,0,1:T(8,128)(2,1)}, bf16[256,4,128]{2,0,1:T(8,128)(2,1)S(1)}, u32[]{:S(2)}) copy-start(bf16[256,4,128]{2,0,1:T(8,128)(2,1)S(1)} %convolution_convert_fusion.8) | copy-start | bytes 786436
  121.1 274.9 %copy-start.10 = (f32[128,1152]{1,0:T(8,128)}, f32[128,1152]{1,0:T(8,128)S(1)}, u32[]{:S(2)}) copy-start(f32[128,1152]{1,0:T(8,128)S(1)} %get-tuple-element.71) | copy-start | bytes 1769476
  121.1 274.9 %copy-start.32 = (f32[128]{0:T(128)}, f32[128]{0:T(128)S(1)}, u32[]{:S(2)}) copy-start(f32[128]{0:T(128)S(1)} %add_rsqrt_fusion.3) | copy-start | bytes 1540
  177.1 5.3 copy-start.39
  177.1 5.3 copy-start.41
  185.3 3.2 copy-start.46
  312.4 4.6 copy-start.11
  312.4 4.6 copy-start.40
  317.0 3.0 copy-start.42
  317.0 3.0 copy-start.44
  324.8 67.9 %all-to-all-start.3 = ((bf16[16,128,1152]{2,1,0:T(8,128)(2,1)}), bf16[16,128,1152]{2,1,0:T(8,128)(2,1)}, u32[]{:S(2)}, u32[]{:S(2)}) async-start(bf16[16,128,1152]{2,1,0:T(8,128)(2,1)} %bitcast.205), calls=%async_computation.3 | async-start | bytes 9437184 | tf_op jit(solution)/shard_map/all_to_all | solution.py:75
  396.5 9.3 %copy-start.8 = (f32[128,1152]{1,0:T(8,128)}, f32[128,1152]{1,0:T(8,128)S(1)}, u32[]{:S(2)}) copy-start(f32[128,1152]{1,0:T(8,128)S(1)} %get-tuple-element.39) | copy-start | bytes 1769476
  396.5 7.4 %copy-start.5 = (f32[1024,128,4]{1,0,2:T(8,128)S(1)}, f32[1024,128,4]{1,0,2:T(8,128)}, u32[]{:S(2)}) copy-start(f32[1024,128,4]{1,0,2:T(8,128)} %copy-done.4) | copy-start | bytes 6291460
  396.5 7.4 %copy-start.31 = (f32[4,128]{1,0:T(4,128)S(1)}, f32[4,128]{1,0:T(4,128)}, u32[]{:S(2)}) copy-start(f32[4,128]{1,0:T(4,128)} %copy-done.30) | copy-start | bytes 6148
  403.9 3.7 copy-start.12
  407.6 7.0 %copy-start.22 = (f32[128,128]{1,0:T(8,128)S(1)}, f32[128,128]{1,0:T(8,128)}, u32[]{:S(2)}) copy-start(f32[128,128]{1,0:T(8,128)} %copy-done.21) | copy-start | bytes 196612
  407.6 7.0 %copy-start.24 = (f32[128,128]{1,0:T(8,128)S(1)}, f32[128,128]{1,0:T(8,128)}, u32[]{:S(2)}) copy-start(f32[128,128]{1,0:T(8,128)} %copy-done.23) | copy-start | bytes 196612
  407.6 8.1 %copy-start.7 = (f32[128,4,256]{2,0,1:T(8,128)S(1)}, f32[128,4,256]{2,0,1:T(8,128)}, u32[]{:S(2)}) copy-start(f32[128,4,256]{2,0,1:T(8,128)} %copy-done.6) | copy-start | bytes 1572868
  409.2 8.9 %copy-start.15 = (bf16[128,1152]{1,0:T(8,128)(2,1)S(1)}, bf16[128,1152]{1,0:T(8,128)(2,1)}, u32[]{:S(2)}) copy-start(bf16[128,1152]{1,0:T(8,128)(2,1)} %copy-done.14) | copy-start | bytes 884740
  409.2 8.9 %copy-start.17 = (bf16[256,4,128]{2,0,1:T(8,128)(2,1)S(1)}, bf16[256,4,128]{2,0,1:T(8,128)(2,1)}, u32[]{:S(2)}) copy-start(bf16[256,4,128]{2,0,1:T(8,128)(2,1)} %copy-done.16) | copy-start | bytes 786436
  409.2 21.0 %all-to-all-start.4 = ((bf16[8,128,512]{2,1,0:T(8,128)(2,1)}), bf16[8,128,512]{2,1,0:T(8,128)(2,1)S(1)}, u32[]{:S(2)}, u32[]{:S(2)}) async-start(bf16[8,128,512]{2,1,0:T(8,128)(2,1)} %pad_maximum_fusion.2), calls=%async_computation.4 | async-start | bytes 2097152 | tf_op jit(solution)/shard_map/all_to_all | solution.py:75
  414.4 159.4 %reduce-scatter.4.cloned.1.call-start = ((), (), s32[]{:S(2)}) async-start(), calls=%async_computation.13 | async-start | bytes 6266880
  418.1 12.2 %copy-start.36 = (f32[128]{0:T(128)S(1)}, f32[128]{0:T(128)}, u32[]{:S(2)}) copy-start(f32[128]{0:T(128)} %copy-done.35) | copy-start | bytes 1540
  418.1 12.2 %copy-start.38 = (f32[128]{0:T(128)S(1)}, f32[128]{0:T(128)}, u32[]{:S(2)}) copy-start(f32[128]{0:T(128)} %copy-done.37) | copy-start | bytes 1540
  418.1 12.9 %copy-start.34 = (f32[128]{0:T(128)S(1)}, f32[128]{0:T(128)}, u32[]{:S(2)}) copy-start(f32[128]{0:T(128)} %copy-done.33) | copy-start | bytes 1540
  445.3 5.5 slice-start
  445.4 5.5 slice-start.1
  445.4 5.5 copy-start.45
  509.9 47.5 %all-to-all-start.9 = ((bf16[8,162,1152]{2,1,0:T(8,128)(2,1)}), bf16[8,162,1152]{2,1,0:T(8,128)(2,1)}, u32[]{:S(2)}, u32[]{:S(2)}) async-start(bf16[8,162,1152]{2,1,0:T(8,128)(2,1)} %broadcast_in_dim.117), calls=%async_computation.9 | async-start | bytes 6193152 | tf_op jit(solution)/shard_map/all_to_all | solution.py:274
  557.4 16.3 %all-to-all-start.5 = ((bf16[16,8,72]{2,1,0:T(8,128)(2,1)}), bf16[16,8,72]{2,1,0:T(8,128)(2,1)S(1)}, u32[]{:S(2)}, u32[]{:S(2)}) async-start(bf16[16,8,72]{2,1,0:T(8,128)(2,1)} %copy.100), calls=%async_computation.5 | async-start | bytes 65536 | tf_op jit(solution)/shard_map/all_to_all | solution.py:269
  576.4 12.5 %all-to-all-start.6 = ((bf16[8,321,72]{1,2,0:T(8,128)(2,1)}), bf16[8,321,72]{1,2,0:T(8,128)(2,1)S(1)}, u32[]{:S(2)}, u32[]{:S(2)}) async-start(bf16[8,321,72]{1,2,0:T(8,128)(2,1)} %copy.102), calls=%async_computation.6 | async-start | bytes 884736 | tf_op jit(solution)/shard_map/all_to_all | solution.py:273
  579.8 13.4 %copy-start.9 = (f32[128,1152]{1,0:T(8,128)S(1)}, f32[128,1152]{1,0:T(8,128)}, u32[]{:S(2)}) copy-start(f32[128,1152]{1,0:T(8,128)} %copy-done.8) | copy-start | bytes 1769476
  589.0 16.0 %copy-start.1 = (bf16[432,1152]{1,0:T(8,128)(2,1)S(1)}, bf16[432,1152]{1,0:T(8,128)(2,1)}, u32[]{:S(2)}) copy-start(bf16[432,1152]{1,0:T(8,128)(2,1)} %param.27) | copy-start | bytes 2985988
  589.8 11.9 %all-to-all-start.7 = ((bf16[8,321,72]{1,2,0:T(8,128)(2,1)}), bf16[8,321,72]{1,2,0:T(8,128)(2,1)S(1)}, u32[]{:S(2)}, u32[]{:S(2)}) async-start(bf16[8,321,72]{1,2,0:T(8,128)(2,1)} %broadcast_in_dim.116), calls=%async_computation.7 | async-start | bytes 884736 | tf_op jit(solution)/shard_map/all_to_all | solution.py:274
  (11 other events, 19.6 us)
Sparse Core Ops, SparseCore 0:
  13.2 66.3 all-gather.2
  122.4 54.6 all-gather.4
  445.5 122.8 reduce-scatter.3
where the time goes:
time: 617 us; the launch traced here: 612 us
  waiting for transfers between devices  248 us (40%)
  blocking collectives  165 us (27%)
  matrix products  61.3 us (10%)
  local copies, waits for them, and re-layouts  55.1 us (9%)
  starting transfers between devices  35.7 us (6%)
  other arithmetic  31.1 us (5%)
  between operations  15.1 us (2%)
    all_to_all x2, waiting for transfers between devices, a2a_sum(): pieces = lax.all_to_all(x.reshape(count, -1, *x.shape[1:]), axis_name, 0, 0)  67.6 us
    all_gather x1, waiting for transfers between devices, body(): packed_all = lax.all_gather(packed, 'fsdp', axis=0, tiled=True)  63.4 us
    all_to_all x1, blocking collectives, a2a_sum(): pieces = lax.all_to_all(x.reshape(count, -1, *x.shape[1:]), axis_name, 0, 0)  60.9 us
    all_to_all x1, blocking collectives, a2a_gather(): lax.all_to_all(copies, axis_name, 0, 0)  60.2 us
    all_gather x1, waiting for transfers between devices, body(): rows_all = lax.all_gather(normed_pre, 'fsdp', axis=0, tiled=True)  54.8 us
    all_to_all x1, blocking collectives, ctx_sum(): lax.all_to_all(chunks, 'ctx', 0, 0).astype(f32)  44.3 us
    all_to_all x2, waiting for transfers between devices, ctx_sum(): lax.all_to_all(jnp.broadcast_to(mine[None], chunks.shape), 'ctx', 0, 0)  43 us
    unnamed x106, local copies, waits for them, and re-layouts  18 us
  transfers between devices with their start and end apart: 10, of which 9 were waited for; matrix products, arithmetic and copies ran while one was open for 9% of the time, Pallas kernels for 0%

commit v1 on v0

--- a/solution.py
+++ b/solution.py
@@ -124,7 +124,9 @@
     )
     gain_cols = jnp.pad(gain_cols, ((0, 0), (0, 128 - gain_cols.shape[1])))
     packed = jnp.concatenate([w_query, w_key, w_value, w_output.T, gain_cols], axis=1)
-    packed_all = lax.all_gather(packed, "fsdp", axis=0, tiled=True)
+    packed_all = jnp.concatenate(
+        lax.all_to_all(jnp.stack([packed] * lax.axis_size("fsdp")), "fsdp", 0, 0), axis=0
+    )
     o1 = qw
     o2 = o1 + kw
     o3 = o2 + kw

time: 617 us -> 647 us (1.049)
  waiting for transfers between devices: 248 us -> 270 us
  starting transfers between devices: 35.7 us -> 44.3 us
    all_to_all x0 -> x1, waiting for transfers between devices: none -> 82.7 us  [body(): lax.all_to_all(jnp.stack([packed] * lax.axis_size('fsdp')), 'fsdp', 0, 0)]
    all_gather x1 -> x0, waiting for transfers between devices: 63.4 us -> none  [body(): packed_all = lax.all_gather(packed, 'fsdp', axis=0, tiled=True)]
    all_to_all x0 -> x1, starting transfers between devices: none -> 8.15 us  [body(): lax.all_to_all(jnp.stack([packed] * lax.axis_size('fsdp')), 'fsdp', 0, 0)]
    unnamed x106 -> x110, local copies, waits for them, and re-layouts: 18 us -> 16.7 us
  transfers between devices with their start and end apart: 10 -> 10, of which waited for: 9 -> 9; matrix products, arithmetic and copies ran while one was open for 9% -> 8% of each run, Pallas kernels for 0% -> 0%
where the time goes in v1:
time: 647 us; the launch traced here: 641 us
  waiting for transfers between devices  270 us (42%)
  blocking collectives  165 us (26%)
  matrix products  60.4 us (9%)
  local copies, waits for them, and re-layouts  56.8 us (9%)
  starting transfers between devices  44.3 us (7%)
  other arithmetic  28.9 us (4%)
  between operations  15.5 us (2%)
    all_to_all x1, waiting for transfers between devices, body(): lax.all_to_all(jnp.stack([packed] * lax.axis_size('fsdp')), 'fsdp', 0, 0)  82.7 us
    all_to_all x2, waiting for transfers between devices, a2a_sum(): pieces = lax.all_to_all(x.reshape(count, -1, *x.shape[1:]), axis_name, 0, 0)  68.3 us
    all_to_all x1, blocking collectives, a2a_sum(): pieces = lax.all_to_all(x.reshape(count, -1, *x.shape[1:]), axis_name, 0, 0)  60.9 us
    all_to_all x1, blocking collectives, a2a_gather(): lax.all_to_all(copies, axis_name, 0, 0)  60.2 us
    all_gather x1, waiting for transfers between devices, body(): rows_all = lax.all_gather(normed_pre, 'fsdp', axis=0, tiled=True)  57.1 us
    all_to_all x1, blocking collectives, ctx_sum(): lax.all_to_all(chunks, 'ctx', 0, 0).astype(f32)  44.3 us
    all_to_all x2, waiting for transfers between devices, ctx_sum(): lax.all_to_all(jnp.broadcast_to(mine[None], chunks.shape), 'ctx', 0, 0)  42.9 us
    unnamed x110, local copies, waits for them, and re-layouts  16.7 us
  transfers between devices with their start and end apart: 10, of which 9 were waited for; matrix products, arithmetic and copies ran while one was open for 8% of the time, Pallas kernels for 0%

profile of v1, /device:TPU:0, one launch (start us, length us, event | category | flops | bytes accessed | tf_op | source)
XLA Modules:
  0.0 640.9 jit_solution(15234414686049648212)
XLA Ops:
  12.2 3.0 stack.67
  15.3 8.1 %all-to-all-start = ((bf16[16,72,2688]{2,1,0:T(8,128)(2,1)}), bf16[16,72,2688]{2,1,0:T(8,128)(2,1)}, u32[]{:S(2)}, u32[]{:S(2)}) async-start(bf16[16,72,2688]{2,1,0:T(8,128)(2,1)} %stack.67), calls=%async_computation | async-start | bytes 12386304 | tf_op jit(solution)/shard_map/all_to_all | solution.py:128
  24.3 82.7 %all-to-all-done = bf16[16,72,2688]{2,1,0:T(8,128)(2,1)} async-done(((bf16[16,72,2688]{2,1,0:T(8,128)(2,1)}), bf16[16,72,2688]{2,1,0:T(8,128)(2,1)}, u32[]{:S(2)}, u32[]{:S(2)}) %all-to-all-start) | async-done | bytes 6193184 | tf_op jit(solution)/shard_map/all_to_all | solution.py:128
  107.9 3.3 slice_bitcast_fusion
  116.0 4.3 copy.103
  122.1 4.8 all-to-all-start.1
  127.4 2.7 multiply_reduce_fusion.10
  131.1 11.7 %all-to-all-done.1 = bf16[8,128,512]{2,1,0:T(8,128)(2,1)S(1)} async-done(((bf16[8,128,512]{2,1,0:T(8,128)(2,1)}), bf16[8,128,512]{2,1,0:T(8,128)(2,1)S(1)}, u32[]{:S(2)}, u32[]{:S(2)}) %all-to-all-start.1) | async-done | bytes 1048608 | tf_op jit(solution)/shard_map/all_to_all | solution.py:81
  145.3 2.8 multiply_reduce_fusion.6
  149.3 57.1 %all-gather.2.cloned.1.call-done = bf16[2048,1152]{1,0:T(8,128)(2,1)} async-done(((bf16[128,1152]{1,0:T(8,128)(2,1)}), bf16[2048,1152]{1,0:T(8,128)(2,1)}) %all-gather.2.cloned.1.call-update) | async-done | bytes 4718608 | tf_op jit(solution)/shard_map/all_gather | solution.py:186
  206.4 5.2 fusion.109
  211.7 2.9 multiply_convert_fusion.1
  214.7 3.2 convolution_convert_fusion
  217.9 60.9 %all_to_all.55 = bf16[16,128,1152]{2,1,0:T(8,128)(2,1)S(1)} all-to-all(bf16[16,128,1152]{2,1,0:T(8,128)(2,1)S(1)} %bitcast.207), channel_id=1, replica_groups=mesh['ctx'=8,'fsdp'=16] {'fsdp'}, dimensions={0} | all-to-all | bytes 9437184 | tf_op jit(solution)/shard_map/all_to_all | solution.py:75
  281.6 60.2 %all_to_all.56 = bf16[16,128,1152]{2,1,0:T(8,128)(2,1)S(1)} all-to-all(bf16[16,128,1152]{2,1,0:T(8,128)(2,1)S(1)} %broadcast_in_dim.66), channel_id=1, replica_groups=mesh['ctx'=8,'fsdp'=16] {'fsdp'}, dimensions={0} | all-to-all | bytes 9437184 | tf_op jit(solution)/shard_map/all_to_all | solution.py:81
  341.7 4.6 multiply_convert_fusion
  346.4 3.0 fusion.110
  349.4 4.8 add_convert_fusion
  354.1 4.6 all-to-all-start.4
  358.9 3.0 fusion.8
  361.9 60.1 %all-to-all-done.4 = bf16[16,128,1152]{2,1,0:T(8,128)(2,1)} async-done(((bf16[16,128,1152]{2,1,0:T(8,128)(2,1)}), bf16[16,128,1152]{2,1,0:T(8,128)(2,1)}, u32[]{:S(2)}, u32[]{:S(2)}) %all-to-all-start.4) | async-done | bytes 4718624 | tf_op jit(solution)/shard_map/all_to_all | solution.py:75
  422.0 3.1 convert_reduce_fusion
  428.1 2.9 fusion.22
  437.9 5.1 all-to-all-start.5
  446.0 2.2 convolution_convert_fusion.1
  448.2 2.3 convolution_convert_fusion.2
  450.5 8.2 %all-to-all-done.5 = bf16[8,128,512]{2,1,0:T(8,128)(2,1)S(1)} async-done(((bf16[8,128,512]{2,1,0:T(8,128)(2,1)}), bf16[8,128,512]{2,1,0:T(8,128)(2,1)S(1)}, u32[]{:S(2)}, u32[]{:S(2)}) %all-to-all-start.5) | async-done | bytes 1048608 | tf_op jit(solution)/shard_map/all_to_all | solution.py:75
  460.4 4.6 pad_maximum_fusion
  465.0 8.9 %copy.130 = bf16[2560,1152]{0,1:T(8,128)(2,1)} copy(bf16[2560,1152]{1,0:T(8,128)(2,1)} %pad_maximum_fusion) | data formatting | bytes 11796480
  474.0 5.5 convolution_convert_fusion.3
  479.5 2.5 convolution_convert_fusion.4
  482.0 2.5 convolution_convert_fusion.5
  484.5 1.8 pad_maximum_fusion.1
  486.3 3.6 convert_element_type.207
  489.9 44.3 %all_to_all.57 = bf16[8,162,1152]{2,1,0:T(8,128)(2,1)} all-to-all(bf16[8,162,1152]{2,1,0:T(8,128)(2,1)} %convert_element_type.207), channel_id=1, replica_groups=mesh['ctx'=8,'fsdp'=16] {'ctx'}, dimensions={0} | all-to-all | bytes 5971968 | tf_op jit(solution)/shard_map/all_to_all | solution.py:275
  534.2 2.4 reduce_sum.291
  536.6 1.9 broadcast_in_dim.117
  538.5 5.3 all-to-all-start.10
  544.0 2.6 fusion.15
  550.6 35.5 %all-to-all-done.10 = bf16[8,162,1152]{2,1,0:T(8,128)(2,1)} async-done(((bf16[8,162,1152]{2,1,0:T(8,128)(2,1)}), bf16[8,162,1152]{2,1,0:T(8,128)(2,1)}, u32[]{:S(2)}, u32[]{:S(2)}) %all-to-all-start.10) | async-done | bytes 2986016 | tf_op jit(solution)/shard_map/all_to_all | solution.py:276
  586.1 8.7 %all-to-all-start.6 = ((bf16[16,8,72]{2,1,0:T(8,128)(2,1)}), bf16[16,8,72]{2,1,0:T(8,128)(2,1)S(1)}, u32[]{:S(2)}, u32[]{:S(2)}) async-start(bf16[16,8,72]{2,1,0:T(8,128)(2,1)} %copy.113), calls=%async_computation.6 | async-start | bytes 65536 | tf_op jit(solution)/shard_map/all_to_all | solution.py:271
  594.9 4.3 reshape.431
  599.2 3.3 all-to-all-done.6
  605.2 3.5 all-to-all-start.7
  608.6 5.5 fusion.107
  614.2 3.5 all-to-all-done.7
  618.6 3.5 all-to-all-start.8
  623.0 7.4 %all-to-all-done.8 = bf16[8,321,72]{1,2,0:T(8,128)(2,1)S(1)} async-done(((bf16[8,321,72]{1,2,0:T(8,128)(2,1)}), bf16[8,321,72]{1,2,0:T(8,128)(2,1)S(1)}, u32[]{:S(2)}, u32[]{:S(2)}) %all-to-all-start.8) | async-done | bytes 369824 | tf_op jit(solution)/shard_map/all_to_all | solution.py:276
  (216 shorter events, 47.7 us)
Async XLA Ops:
  7.2 207.5 %copy-start = (bf16[432,1152]{1,0:T(8,128)(2,1)S(1)}, bf16[432,1152]{1,0:T(8,128)(2,1)}, u32[]{:S(2)}) copy-start(bf16[432,1152]{1,0:T(8,128)(2,1)} %param.27) | copy-start | bytes 2985988
  15.2 8.2 %copy-start.39 = (s32[8,2]{0,1:T(2,128)S(1)}, s32[8,2]{0,1:T(2,128)}, u32[]{:S(2)}) copy-start(s32[8,2]{0,1:T(2,128)} %param.20) | copy-start | bytes 196
  15.3 8.6 %copy-start.2 = (bf16[1,128,1152]{2,1,0:T(8,128)(2,1)S(1)}, bf16[1,128,1152]{2,1,0:T(8,128)(2,1)}, u32[]{:S(2)}) copy-start(bf16[1,128,1152]{2,1,0:T(8,128)(2,1)} %param.17) | copy-start | bytes 884740
  15.3 8.7 %copy-start.43 = (s32[1,128]{1,0:T(1,128)S(1)}, s32[1,128]{1,0:T(1,128)}, u32[]{:S(2)}) copy-start(s32[1,128]{1,0:T(1,128)} %param.19) | copy-start | bytes 1540
  15.3 91.7 %all-to-all-start = ((bf16[16,72,2688]{2,1,0:T(8,128)(2,1)}), bf16[16,72,2688]{2,1,0:T(8,128)(2,1)}, u32[]{:S(2)}, u32[]{:S(2)}) async-start(bf16[16,72,2688]{2,1,0:T(8,128)(2,1)} %stack.67), calls=%async_computation | async-start | bytes 12386304 | tf_op jit(solution)/shard_map/all_to_all | solution.py:128
  23.6 97.0 %copy-start.34 = (f32[128]{0:T(128)}, f32[128]{0:T(128)S(1)}, u32[]{:S(2)}) copy-start(f32[128]{0:T(128)S(1)} %multiply_power_fusion) | copy-start | bytes 1540
  24.0 96.6 %copy-start.36 = (f32[128]{0:T(128)}, f32[128]{0:T(128)S(1)}, u32[]{:S(2)}) copy-start(f32[128]{0:T(128)S(1)} %convert_bitcast_fusion.2) | copy-start | bytes 1540
  24.2 119.5 %copy-start.24 = (pred[128,1024]{0,1:T(8,128)(4,1)}, pred[128,1024]{0,1:T(8,128)(4,1)S(1)}, u32[]{:S(2)}) copy-start(pred[128,1024]{0,1:T(8,128)(4,1)S(1)} %broadcast_compare_fusion.1) | copy-start | bytes 393220
  115.8 6.2 copy-start.32
  120.9 10.1 %copy-start.20 = (f32[128,128]{1,0:T(8,128)}, f32[128,128]{1,0:T(8,128)S(1)}, u32[]{:S(2)}) copy-start(f32[128,128]{1,0:T(8,128)S(1)} %get-tuple-element.60) | copy-start | bytes 196612
  121.0 10.1 %copy-start.22 = (f32[128,128]{1,0:T(8,128)}, f32[128,128]{1,0:T(8,128)S(1)}, u32[]{:S(2)}) copy-start(f32[128,128]{1,0:T(8,128)S(1)} %get-tuple-element.61) | copy-start | bytes 196612
  122.1 20.8 %all-to-all-start.1 = ((bf16[8,128,512]{2,1,0:T(8,128)(2,1)}), bf16[8,128,512]{2,1,0:T(8,128)(2,1)S(1)}, u32[]{:S(2)}, u32[]{:S(2)}) async-start(bf16[8,128,512]{2,1,0:T(8,128)(2,1)} %broadcast_in_dim.56), calls=%async_computation.1 | async-start | bytes 2097152 | tf_op jit(solution)/shard_map/all_to_all | solution.py:81
  126.8 79.6 %all-gather.2.cloned.1.call-start = ((), (), s32[]{:S(2)}) async-start(), calls=%async_computation.12 | async-start | bytes 5013504 | tf_op jit(solution)/shard_map/all_gather | solution.py:186
  131.1 12.7 %copy-start.25 = (f32[128,4,128]{2,0,1:T(8,128)}, f32[128,4,128]{2,0,1:T(8,128)S(1)}, u32[]{:S(2)}) copy-start(f32[128,4,128]{2,0,1:T(8,128)S(1)} %get-tuple-element.53) | copy-start | bytes 786436
  131.1 14.2 %copy-start.27 = (f32[128,4,128]{2,0,1:T(8,128)}, f32[128,4,128]{2,0,1:T(8,128)S(1)}, u32[]{:S(2)}) copy-start(f32[128,4,128]{2,0,1:T(8,128)S(1)} %get-tuple-element.54) | copy-start | bytes 786436
  144.6 214.3 %copy-start.29 = (f32[4,128]{1,0:T(4,128)}, f32[4,128]{1,0:T(4,128)S(1)}, u32[]{:S(2)}) copy-start(f32[4,128]{1,0:T(4,128)S(1)} %log_add_fusion) | copy-start | bytes 6148
  145.3 66.3 %copy-start.16 = (bf16[256,4,128]{2,0,1:T(8,128)(2,1)}, bf16[256,4,128]{2,0,1:T(8,128)(2,1)S(1)}, u32[]{:S(2)}) copy-start(bf16[256,4,128]{2,0,1:T(8,128)(2,1)S(1)} %convolution_convert_fusion.8) | copy-start | bytes 786436
  148.1 277.3 %copy-start.10 = (f32[128,1152]{1,0:T(8,128)}, f32[128,1152]{1,0:T(8,128)S(1)}, u32[]{:S(2)}) copy-start(f32[128,1152]{1,0:T(8,128)S(1)} %get-tuple-element.71) | copy-start | bytes 1769476
  148.1 277.3 %copy-start.31 = (f32[128]{0:T(128)}, f32[128]{0:T(128)S(1)}, u32[]{:S(2)}) copy-start(f32[128]{0:T(128)S(1)} %add_rsqrt_fusion.3) | copy-start | bytes 1540
  206.4 5.3 copy-start.40
  206.4 5.3 copy-start.42
  214.6 3.2 copy-start.48
  341.7 4.6 copy-start.11
  341.7 4.6 copy-start.41
  346.3 3.0 copy-start.44
  346.3 3.0 copy-start.46
  354.1 67.9 %all-to-all-start.4 = ((bf16[16,128,1152]{2,1,0:T(8,128)(2,1)}), bf16[16,128,1152]{2,1,0:T(8,128)(2,1)}, u32[]{:S(2)}, u32[]{:S(2)}) async-start(bf16[16,128,1152]{2,1,0:T(8,128)(2,1)} %bitcast.206), calls=%async_computation.4 | async-start | bytes 9437184 | tf_op jit(solution)/shard_map/all_to_all | solution.py:75
  425.8 9.2 %copy-start.8 = (f32[128,1152]{1,0:T(8,128)}, f32[128,1152]{1,0:T(8,128)S(1)}, u32[]{:S(2)}) copy-start(f32[128,1152]{1,0:T(8,128)S(1)} %get-tuple-element.39) | copy-start | bytes 1769476
  425.8 7.4 %copy-start.5 = (f32[1024,128,4]{1,0,2:T(8,128)S(1)}, f32[1024,128,4]{1,0,2:T(8,128)}, u32[]{:S(2)}) copy-start(f32[1024,128,4]{1,0,2:T(8,128)} %copy-done.4) | copy-start | bytes 6291460
  425.9 7.4 %copy-start.30 = (f32[4,128]{1,0:T(4,128)S(1)}, f32[4,128]{1,0:T(4,128)}, u32[]{:S(2)}) copy-start(f32[4,128]{1,0:T(4,128)} %copy-done.29) | copy-start | bytes 6148
  436.1 7.1 %copy-start.7 = (f32[128,4,256]{2,0,1:T(8,128)S(1)}, f32[128,4,256]{2,0,1:T(8,128)}, u32[]{:S(2)}) copy-start(f32[128,4,256]{2,0,1:T(8,128)} %copy-done.6) | copy-start | bytes 1572868
  436.8 9.2 %copy-start.15 = (bf16[128,1152]{1,0:T(8,128)(2,1)S(1)}, bf16[128,1152]{1,0:T(8,128)(2,1)}, u32[]{:S(2)}) copy-start(bf16[128,1152]{1,0:T(8,128)(2,1)} %copy-done.14) | copy-start | bytes 884740
  436.8 9.2 %copy-start.17 = (bf16[256,4,128]{2,0,1:T(8,128)(2,1)S(1)}, bf16[256,4,128]{2,0,1:T(8,128)(2,1)}, u32[]{:S(2)}) copy-start(bf16[256,4,128]{2,0,1:T(8,128)(2,1)} %copy-done.16) | copy-start | bytes 786436
  437.9 20.9 %all-to-all-start.5 = ((bf16[8,128,512]{2,1,0:T(8,128)(2,1)}), bf16[8,128,512]{2,1,0:T(8,128)(2,1)S(1)}, u32[]{:S(2)}, u32[]{:S(2)}) async-start(bf16[8,128,512]{2,1,0:T(8,128)(2,1)} %pad_maximum_fusion.2), calls=%async_computation.5 | async-start | bytes 2097152 | tf_op jit(solution)/shard_map/all_to_all | solution.py:75
  442.9 159.6 %reduce-scatter.4.cloned.1.call-start = ((), (), s32[]{:S(2)}) async-start(), calls=%async_computation.13 | async-start | bytes 6266880
  446.0 12.9 %copy-start.35 = (f32[128]{0:T(128)S(1)}, f32[128]{0:T(128)}, u32[]{:S(2)}) copy-start(f32[128]{0:T(128)} %copy-done.34) | copy-start | bytes 1540
  446.0 12.9 %copy-start.37 = (f32[128]{0:T(128)S(1)}, f32[128]{0:T(128)}, u32[]{:S(2)}) copy-start(f32[128]{0:T(128)} %copy-done.36) | copy-start | bytes 1540
  446.0 13.7 %copy-start.33 = (f32[128]{0:T(128)S(1)}, f32[128]{0:T(128)}, u32[]{:S(2)}) copy-start(f32[128]{0:T(128)} %copy-done.32) | copy-start | bytes 1540
  473.9 5.5 slice-start
  473.9 5.5 slice-start.1
  474.0 5.5 copy-start.47
  538.5 5.3 copy-start.38
  538.5 47.7 %all-to-all-start.10 = ((bf16[8,162,1152]{2,1,0:T(8,128)(2,1)}), bf16[8,162,1152]{2,1,0:T(8,128)(2,1)}, u32[]{:S(2)}, u32[]{:S(2)}) async-start(bf16[8,162,1152]{2,1,0:T(8,128)(2,1)} %broadcast_in_dim.117), calls=%async_computation.10 | async-start | bytes 6193152 | tf_op jit(solution)/shard_map/all_to_all | solution.py:276
  586.1 16.3 %all-to-all-start.6 = ((bf16[16,8,72]{2,1,0:T(8,128)(2,1)}), bf16[16,8,72]{2,1,0:T(8,128)(2,1)S(1)}, u32[]{:S(2)}, u32[]{:S(2)}) async-start(bf16[16,8,72]{2,1,0:T(8,128)(2,1)} %copy.113), calls=%async_computation.6 | async-start | bytes 65536 | tf_op jit(solution)/shard_map/all_to_all | solution.py:271
  605.2 12.5 %all-to-all-start.7 = ((bf16[8,321,72]{1,2,0:T(8,128)(2,1)}), bf16[8,321,72]{1,2,0:T(8,128)(2,1)S(1)}, u32[]{:S(2)}, u32[]{:S(2)}) async-start(bf16[8,321,72]{1,2,0:T(8,128)(2,1)} %copy.115), calls=%async_computation.7 | async-start | bytes 884736 | tf_op jit(solution)/shard_map/all_to_all | solution.py:275
  608.6 13.4 %copy-start.9 = (f32[128,1152]{1,0:T(8,128)S(1)}, f32[128,1152]{1,0:T(8,128)}, u32[]{:S(2)}) copy-start(f32[128,1152]{1,0:T(8,128)} %copy-done.8) | copy-start | bytes 1769476
  617.8 16.0 %copy-start.1 = (bf16[432,1152]{1,0:T(8,128)(2,1)S(1)}, bf16[432,1152]{1,0:T(8,128)(2,1)}, u32[]{:S(2)}) copy-start(bf16[432,1152]{1,0:T(8,128)(2,1)} %param.27) | copy-start | bytes 2985988
  618.6 11.9 %all-to-all-start.8 = ((bf16[8,321,72]{1,2,0:T(8,128)(2,1)}), bf16[8,321,72]{1,2,0:T(8,128)(2,1)S(1)}, u32[]{:S(2)}, u32[]{:S(2)}) async-start(bf16[8,321,72]{1,2,0:T(8,128)(2,1)} %broadcast_in_dim.116), calls=%async_computation.8 | async-start | bytes 884736 | tf_op jit(solution)/shard_map/all_to_all | solution.py:276
  (13 other events, 25.1 us)
Sparse Core Ops, SparseCore 0:
  149.4 56.9 all-gather.1
  474.1 122.4 reduce-scatter.3
